TPU v7x, 32 devices: a whole 2x2x4 slice. The times are simulated.
32 devices in a mesh: ctx: 8 (over y, x, core), wa: 4 (over z).
Axes of the slice: x: 2, y: 2, z: 4, core: 2. Of those that a mesh axis runs over, the one named last changes fastest.
Arguments:
- block_input: bfloat16 [1024, 1088], P('ctx'), may hold values from -6 to 6
- span_table: int32 [8, 2], replicated, may hold values from 0 to 15, as said below
- doc_ids: int32 [1024], replicated, may hold values from 0 to 3, never falling along the last dimension, each value on 1 to 512 neighbouring positions
- attn_gain: float32 [1088], replicated, may hold values from 0.5 to 1.5
- attn_shift: float32 [1088], replicated, may hold values from -1.75 to 1.75
- qkv_weight: bfloat16 [1088, 3264], P('wa'), may hold values from -0.1875 to 0.1875
- query_bias: float32 [1088], replicated, may hold values from -3 to 3
- value_bias: float32 [1088], replicated, may hold values from -3 to 3
- out_weight: bfloat16 [1088, 1088], P(None, 'wa'), may hold values from -1 to 1
- out_bias: float32 [1088], replicated, may hold values from -3 to 3
- mlp_gain: float32 [1088], replicated, may hold values from 0.1 to 1.9
- mlp_shift: float32 [1088], replicated, may hold values from -1.75 to 1.75
- up_weight: bfloat16 [1088, 4352], P(None, 'wa'), may hold values from -0.1875 to 0.1875
- up_bias: float32 [4352], P('wa'), may hold values from -3 to 3
- down_weight: bfloat16 [4352, 1088], P('wa'), may hold values from -0.09375 to 0.09375
- down_bias: float32 [1088], replicated, may hold values from -6 to 6
- cotangent: bfloat16 [1024, 1088], P('ctx'), may hold values from -6 to 6
Outputs:
- block_output: bfloat16 [1024, 1088], P('ctx', 'wa')
- input_grad: bfloat16 [1024, 1088], P('ctx')
- qkv_grad: float32 [1088, 3264], P('wa', 'ctx')
- query_bias_grad: float32 [1088], replicated
- value_bias_grad: float32 [1088], replicated
- out_grad: float32 [1088, 1088], P('ctx', 'wa')
- out_bias_grad: float32 [1088], replicated
- up_grad: float32 [1088, 4352], P('ctx', 'wa')
- up_bias_grad: float32 [4352], P('wa')
- down_grad: float32 [4352, 1088], P('wa', 'ctx')
- down_bias_grad: float32 [1088], replicated
- attn_gain_grad: float32 [1088], replicated
- attn_shift_grad: float32 [1088], replicated
- mlp_gain_grad: float32 [1088], replicated
- mlp_shift_grad: float32 [1088], replicated
Inputs may be any that keep to these rules, and one draw needn't show every extreme that they name: The spans of 64 tokens are numbered in sequence order; the two spans of each row of span_table have numbers that add up to the count of spans minus one, and every span stands in exactly one row. `doc_ids`: document numbers never fall along the sequence; each document holds at most 512 tokens.
All inputs are finite; a program needn't handle non-finite values.
Results may differ from a plain program's by a relative error of at most 0.033.
Values may be sent and summed in bfloat16 or wider, within the bound.
No kernel may reach another device: no remote copies, remote signals or barrier semaphores. Data moves between devices by JAX's collectives and lax.ppermute only.
A program may use at most 320 MiB of HBM per device.

v0:
```python
import jax
import jax.numpy as jnp
from jax import lax
from jax.sharding import PartitionSpec as P

HEADS = 17
HEAD_DIM = 64
TOK_CTX = 128
SPAN = 64
norm_eps = 1e-05
root_half = 0.7071067811865476
inv_root_tau = 0.3989422804014327


def rounded(value):
    return lax.optimization_barrier(value.astype(jnp.bfloat16))


def gelu_value(pre):
    return 0.5 * pre * (1.0 + lax.erf(pre * root_half))


def gelu_slope(pre):
    return 0.5 * (1.0 + lax.erf(pre * root_half)) + pre * inv_root_tau * jnp.exp(-0.5 * pre * pre)


def norm_parts(values, gain, shift):
    center = jnp.mean(values, axis=-1, keepdims=True)
    square = jnp.mean(values * values, axis=-1, keepdims=True)
    inv_std = lax.rsqrt(square - center * center + norm_eps)
    normed = (values - center) * inv_std
    return (normed, inv_std, normed * gain + shift)


def norm_back(grad_out, normed, inv_std, gain):
    scaled = grad_out * gain
    return inv_std * (
        scaled
        - jnp.mean(scaled, axis=-1, keepdims=True)
        - normed * jnp.mean(scaled * normed, axis=-1, keepdims=True)
    )


def contract_rows(left, right):
    return lax.dot_general(
        left, right, (((0,), (0,)), ((), ())), preferred_element_type=jnp.float32
    )


def contract_cols(left, right):
    return lax.dot_general(
        left, right, (((1,), (1,)), ((), ())), preferred_element_type=jnp.float32
    )


def token_places(row_ids, span_table, doc_ids):
    owner = row_ids // TOK_CTX
    halves = row_ids % TOK_CTX // SPAN
    places = span_table[owner, halves] * SPAN + row_ids % SPAN
    return (places, doc_ids[places])


def body(
    block_input,
    span_table,
    doc_ids,
    attn_gain,
    attn_shift,
    qkv_weight,
    query_bias,
    value_bias,
    out_weight,
    out_bias,
    mlp_gain,
    mlp_shift,
    up_weight,
    up_bias,
    down_weight,
    down_bias,
    cotangent,
):
    tok_rows, model_width = block_input.shape
    wa_count = lax.axis_size("wa")
    wa_index = lax.axis_index("wa")
    ctx_index = lax.axis_index("ctx")
    col_width = model_width // wa_count
    col_start = wa_index * col_width
    score_scale = float(HEAD_DIM) ** (-0.5)
    input_f = block_input.astype(jnp.float32)
    attn_hat, attn_inv, attn_norm = norm_parts(input_f, attn_gain, attn_shift)
    normed_in = attn_norm.astype(jnp.bfloat16)
    normed_cols = lax.dynamic_slice_in_dim(normed_in, col_start, col_width, 1)
    bias_row = jnp.concatenate([query_bias, jnp.zeros_like(query_bias), value_bias])
    head_count = HEADS
    rows_here = tok_rows // wa_count
    first_row = (ctx_index * wa_count + wa_index) * rows_here
    query_index = first_row + jnp.arange(rows_here, dtype=jnp.int32)

    def row_sums(term_fn):
        return lax.psum_scatter(
            term_fn(jnp.int32(0), lax.axis_size("wa") * rows_here).astype(jnp.bfloat16),
            "wa",
            scatter_dimension=0,
            tiled=True,
        ).astype(jnp.float32)

    def row_gather(piece):
        return lax.all_gather(piece, "wa", axis=0, tiled=True)

    def qkv_term(offset, piece_len):
        return jnp.dot(normed_cols, qkv_weight, preferred_element_type=jnp.float32)

    qkv_own = (row_sums(qkv_term) + bias_row).astype(jnp.bfloat16)
    queries = qkv_own[:, :model_width]
    key_rows = qkv_own[:, model_width : 2 * model_width]
    val_rows = qkv_own[:, 2 * model_width :]

    def fold_keys(fold_fn, init):
        return fold_fn(
            init,
            (
                lax.all_gather(key_rows, ("ctx", "wa"), axis=0, tiled=True),
                lax.all_gather(val_rows, ("ctx", "wa"), axis=0, tiled=True),
            ),
            jnp.int32(0),
        )

    query_place, query_doc = token_places(query_index, span_table, doc_ids)
    query_heads = queries.reshape(rows_here, head_count, HEAD_DIM)

    def key_mask(key_index):
        key_place, key_doc = token_places(key_index, span_table, doc_ids)
        return (key_doc[None, :] == query_doc[:, None]) & (
            key_place[None, :] <= query_place[:, None]
        )

    def attend_piece(softmax_state, pieces, offset):
        row_top, row_total, out_accum = softmax_state
        key_piece, val_piece = pieces
        piece_len = key_piece.shape[0]
        allowed = key_mask(jnp.arange(piece_len, dtype=jnp.int32))
        scores = (
            jnp.einsum(
                "qhd,khd->hqk",
                query_heads,
                key_piece.reshape(piece_len, head_count, HEAD_DIM),
                preferred_element_type=jnp.float32,
            )
            * score_scale
        )
        scores = jnp.where(allowed[None], scores, -jnp.inf)
        new_top = jnp.maximum(row_top, jnp.max(scores, axis=-1))
        factor = jnp.exp(row_top - new_top)
        exp_scores = jnp.exp(scores - new_top[..., None])
        row_total = jnp.sum(exp_scores, axis=-1)
        piece_out = jnp.einsum(
            "hqk,khd->qhd",
            exp_scores.astype(jnp.bfloat16),
            val_piece.reshape(piece_len, head_count, HEAD_DIM),
            preferred_element_type=jnp.float32,
        )
        out_accum = out_accum * factor.T[..., None] + piece_out
        return (new_top, row_total, out_accum)

    init_state = (
        jnp.full((head_count, rows_here), -1e30, jnp.float32),
        jnp.zeros((head_count, rows_here), jnp.float32),
        jnp.zeros((rows_here, head_count, HEAD_DIM), jnp.float32),
    )
    row_top, row_total, out_accum = fold_keys(attend_piece, init_state)
    attn_out = rounded(
        (out_accum / row_total.T[..., None]).reshape(rows_here, head_count * HEAD_DIM)
    )
    log_norm = (row_top + jnp.log(row_total)).T
    attn_full = row_gather(attn_out)
    out_cols = lax.dynamic_slice_in_dim(out_bias, col_start, col_width, 0)
    input_cols = lax.dynamic_slice_in_dim(input_f, col_start, col_width, 1)
    resid_cols = (
        input_cols + jnp.dot(attn_full, out_weight, preferred_element_type=jnp.float32) + out_cols
    )
    resid_full = lax.all_gather(resid_cols.astype(jnp.bfloat16), "wa", axis=1, tiled=True).astype(
        resid_cols.dtype
    )
    mlp_hat, mlp_inv, mlp_norm = norm_parts(resid_full, mlp_gain, mlp_shift)
    normed_mid = mlp_norm.astype(jnp.bfloat16)
    hidden_pre = jnp.dot(normed_mid, up_weight, preferred_element_type=jnp.float32) + up_bias
    hidden_act = gelu_value(hidden_pre).astype(jnp.bfloat16)
    down_part = jnp.dot(hidden_act, down_weight, preferred_element_type=jnp.float32)
    down_cols = lax.psum_scatter(
        down_part.astype(jnp.bfloat16), "wa", scatter_dimension=1, tiled=True
    ).astype(jnp.float32)
    bias_cols = lax.dynamic_slice_in_dim(down_bias, col_start, col_width, 0)
    block_output = (resid_cols + down_cols + bias_cols).astype(jnp.bfloat16)
    grad_f = cotangent.astype(jnp.float32)
    down_bias_part = jnp.sum(grad_f, axis=0)
    down_grad_loc = contract_rows(hidden_act, cotangent)
    hidden_grad = contract_cols(cotangent, down_weight) * gelu_slope(hidden_pre)
    up_bias_part = jnp.sum(hidden_grad, axis=0)
    hidden_grad_b = hidden_grad.astype(jnp.bfloat16)
    up_grad_loc = contract_rows(hidden_grad_b, normed_mid)
    mid_grad = lax.psum(contract_cols(hidden_grad_b, up_weight).astype(jnp.bfloat16), "wa").astype(
        jnp.float32
    )
    mlp_gain_part = jnp.sum(mid_grad * mlp_hat, axis=0)
    mlp_shift_part = jnp.sum(mid_grad, axis=0)
    resid_grad = grad_f + norm_back(mid_grad, mlp_hat, mlp_inv, mlp_gain)
    out_bias_part = jnp.sum(resid_grad, axis=0)
    resid_grad_b = resid_grad.astype(jnp.bfloat16)
    grad_cols = lax.dynamic_slice_in_dim(resid_grad_b, col_start, col_width, 1)
    out_grad_loc = contract_rows(grad_cols, attn_full)

    def attn_term(offset, piece_len):
        return contract_cols(grad_cols, out_weight)

    attn_grad = rounded(row_sums(attn_term))
    grad_heads = attn_grad.reshape(rows_here, head_count, HEAD_DIM)
    out_heads = attn_out.reshape(rows_here, head_count, HEAD_DIM)
    delta = jnp.sum(grad_heads.astype(jnp.float32) * out_heads.astype(jnp.float32), axis=-1)
    log_hi = rounded(log_norm)
    log_lo = rounded(log_norm - log_hi.astype(jnp.float32))
    log_sent = log_hi.astype(jnp.float32) + log_lo.astype(jnp.float32)
    delta_hi = rounded(delta)
    delta_lo = rounded(delta - delta_hi.astype(jnp.float32))
    delta_sent = delta_hi.astype(jnp.float32) + delta_lo.astype(jnp.float32)

    def query_grad_piece(grad_acc, pieces, offset):
        key_piece, val_piece = pieces
        piece_len = key_piece.shape[0]
        allowed = key_mask(jnp.arange(piece_len, dtype=jnp.int32))
        key_heads = key_piece.reshape(piece_len, head_count, HEAD_DIM)
        scores = (
            jnp.einsum("qhd,khd->hqk", query_heads, key_heads, preferred_element_type=jnp.float32)
            * score_scale
        )
        exp_scores = jnp.exp(jnp.where(allowed[None], scores - log_sent.T[..., None], -jnp.inf))
        slopes = jnp.einsum(
            "qhd,khd->hqk",
            grad_heads,
            val_piece.reshape(piece_len, head_count, HEAD_DIM),
            preferred_element_type=jnp.float32,
        )
        score_grad = (exp_scores * (slopes - delta_sent.T[..., None])).astype(jnp.bfloat16)
        return jnp.einsum("hqk,khd->qhd", score_grad, key_heads, preferred_element_type=jnp.float32)

    zero_heads = jnp.zeros((rows_here, head_count, HEAD_DIM), jnp.float32)
    query_grad = fold_keys(query_grad_piece, zero_heads)
    own_keys = key_rows.reshape(rows_here, head_count, HEAD_DIM)
    own_vals = val_rows.reshape(rows_here, head_count, HEAD_DIM)
    pieces = (queries, attn_grad, log_hi, log_lo, delta_hi, delta_lo)
    query_piece = lax.all_gather(pieces[0], ("ctx", "wa"), axis=0, tiled=True)
    grad_piece = lax.all_gather(pieces[1], ("ctx", "wa"), axis=0, tiled=True)
    log_high = lax.all_gather(pieces[2], ("ctx", "wa"), axis=0, tiled=True)
    log_low = lax.all_gather(pieces[3], ("ctx", "wa"), axis=0, tiled=True)
    delta_high = lax.all_gather(pieces[4], ("ctx", "wa"), axis=0, tiled=True)
    delta_low = lax.all_gather(pieces[5], ("ctx", "wa"), axis=0, tiled=True)
    piece_len = query_piece.shape[0]
    piece_place, piece_doc = token_places(
        jnp.arange(piece_len, dtype=jnp.int32), span_table, doc_ids
    )
    allowed = (query_doc[None, :] == piece_doc[:, None]) & (
        query_place[None, :] <= piece_place[:, None]
    )
    piece_heads = query_piece.reshape(piece_len, head_count, HEAD_DIM)
    piece_grads = grad_piece.reshape(piece_len, head_count, HEAD_DIM)
    piece_log = log_high.astype(jnp.float32) + log_low.astype(jnp.float32)
    piece_delta = delta_high.astype(jnp.float32) + delta_low.astype(jnp.float32)
    scores = (
        jnp.einsum("qhd,khd->hqk", piece_heads, own_keys, preferred_element_type=jnp.float32)
        * score_scale
    )
    exp_scores = jnp.exp(jnp.where(allowed[None], scores - piece_log.T[..., None], -jnp.inf))
    slopes = jnp.einsum("qhd,khd->hqk", piece_grads, own_vals, preferred_element_type=jnp.float32)
    score_grad = (exp_scores * (slopes - piece_delta.T[..., None])).astype(jnp.bfloat16)
    key_acc = jnp.einsum(
        "hqk,qhd->khd", score_grad, piece_heads, preferred_element_type=jnp.float32
    )
    val_acc = jnp.einsum(
        "hqk,qhd->khd",
        exp_scores.astype(jnp.bfloat16),
        piece_grads,
        preferred_element_type=jnp.float32,
    )
    here_cols = head_count * HEAD_DIM
    qkv_grad_own = jnp.concatenate(
        [
            (query_grad * score_scale).reshape(rows_here, here_cols),
            (key_acc * score_scale).reshape(rows_here, here_cols),
            val_acc.reshape(rows_here, here_cols),
        ],
        axis=1,
    ).astype(jnp.bfloat16)
    qkv_grad_full = row_gather(qkv_grad_own)
    grad_sums = jnp.sum(qkv_grad_full, axis=0, dtype=jnp.float32)
    query_bias_part = grad_sums[:model_width]
    value_bias_part = grad_sums[2 * model_width :]
    qkv_grad_loc = contract_rows(normed_cols, qkv_grad_full)
    normed_grad_cols = contract_cols(qkv_grad_full, qkv_weight)
    normed_grad = lax.all_gather(
        normed_grad_cols.astype(jnp.bfloat16), "wa", axis=1, tiled=True
    ).astype(normed_grad_cols.dtype)
    attn_gain_part = jnp.sum(normed_grad * attn_hat, axis=0)
    attn_shift_part = jnp.sum(normed_grad, axis=0)
    input_grad = (resid_grad + norm_back(normed_grad, attn_hat, attn_inv, attn_gain)).astype(
        jnp.bfloat16
    )
    qkv_grad_out, out_grad_turned, up_grad_turned, down_grad_out = (
        lax.psum_scatter(qkv_grad_loc, "ctx", scatter_dimension=1, tiled=True),
        lax.psum_scatter(out_grad_loc, "ctx", scatter_dimension=1, tiled=True),
        lax.psum_scatter(up_grad_loc, "ctx", scatter_dimension=1, tiled=True),
        lax.psum_scatter(down_grad_loc, "ctx", scatter_dimension=1, tiled=True),
    )
    packed = jnp.stack(
        [
            attn_gain_part,
            attn_shift_part,
            mlp_gain_part,
            mlp_shift_part,
            query_bias_part,
            value_bias_part,
            out_bias_part,
            down_bias_part,
        ]
    )
    packed_sum, up_bias_grad = lax.psum((packed, up_bias_part), "ctx")
    return (
        block_output,
        input_grad,
        qkv_grad_out,
        packed_sum[4],
        packed_sum[5],
        out_grad_turned.T,
        packed_sum[6],
        up_grad_turned.T,
        up_bias_grad,
        down_grad_out,
        packed_sum[7],
        packed_sum[0],
        packed_sum[1],
        packed_sum[2],
        packed_sum[3],
    )


def solution(mesh):
    placed = (
        P("ctx", None),
        P(),
        P(),
        P(),
        P(),
        P("wa", None),
        P(),
        P(),
        P(None, "wa"),
        P(),
        P(),
        P(),
        P(None, "wa"),
        P("wa"),
        P("wa", None),
        P(),
        P("ctx", None),
    )
    return jax.shard_map(
        body,
        mesh=mesh,
        in_specs=placed,
        out_specs=(
            P("ctx", "wa"),
            P("ctx", None),
            P("wa", "ctx"),
            P(),
            P(),
            P("ctx", "wa"),
            P(),
            P("ctx", "wa"),
            P("wa"),
            P("wa", "ctx"),
            P(),
            P(),
            P(),
            P(),
            P(),
        ),
        check_vma=False,
    )
```

profile of v0, /device:TPU:0, one launch (start us, length us, event | category | flops | bytes accessed | tf_op | source)
XLA Modules:
  0.0 826.9 jit_solution(8947178412588258652)
XLA Ops:
  7.2 1.3 convert_reduce_fusion.5
  8.5 0.8 dynamic-slice.9
  9.3 0.8 dynamic-slice.8
  10.7 1.0 subtract_multiply_fusion
  11.7 0.8 copy-done.15
  12.5 3.2 convolution_convert_fusion
  15.9 26.9 %reduce-scatter.14.cloned.1.call-done = bf16[32,3264]{1,0:T(8,128)(2,1)} async-done(((bf16[128,3264]{1,0:T(8,128)(2,1)}), bf16[32,3264]{1,0:T(8,128)(2,1)}) %reduce-scatter.14.cloned.1.call-update) | async-done | bytes 208912 | tf_op jit(solution)/shard_map/reduce_scatter | solution.py:100
  42.8 1.0 add_convert_fusion
  45.3 0.8 convert_element_type.134
  46.2 0.8 dynamic_slice.17
  47.0 8.8 %gather_fusion = s32[1024]{0:T(1024)S(1)} fusion(s32[8,2]{0,1:T(2,128)S(1)} %copy-done.1, s32[1024]{0:T(1024)S(1)} %bitcast.86), kind=kCustom, calls=%fused_computation | custom fusion | bytes 16384 | tf_op jit(solution)/shard_map/gather | solution.py:59
  55.9 0.8 gather_fusion.2
  56.7 4.5 gather_fusion.1
  62.2 40.2 %all-gather.9.cloned.1.call-done = bf16[1024,1088]{1,0:T(8,128)(2,1)} async-done(((bf16[32,1088]{1,0:T(8,128)(2,1)}), bf16[1024,1088]{1,0:T(8,128)(2,1)}) %all-gather.9.cloned.1.call-update) | async-done | bytes 2228240 | tf_op jit(solution)/shard_map/all_gather | solution.py:122
  102.5 4.2 copy.66
  106.7 2.4 select_reduce_fusion
  109.1 1.4 copy-done.4
  111.1 50.1 %all-gather.11.cloned.1.call-done = bf16[1024,1088]{1,0:T(8,128)(2,1)} async-done(((bf16[32,1088]{1,0:T(8,128)(2,1)}), bf16[1024,1088]{1,0:T(8,128)(2,1)}) %all-gather.11.cloned.1.call-update) | async-done | bytes 2228240 | tf_op jit(solution)/shard_map/all_gather | solution.py:123
  161.1 4.3 copy.68
  165.4 3.2 fusion.11
  168.8 14.0 %all_gather.40 = bf16[128,1088]{1,0:T(8,128)(2,1)S(1)} all-gather(bf16[32,1088]{1,0:T(8,128)(2,1)S(1)} %convert_element_type.141), channel_id=1, replica_groups=mesh['ctx'=8,'wa'=4] {'wa'}, dimensions={0}, use_global_device_ids=true | all-gather | bytes 348160 | tf_op jit(solution)/shard_map/all_gather | solution.py:108
  182.9 2.0 fusion.121
  184.9 14.1 %all_gather.41 = bf16[128,1088]{0,1:T(8,128)(2,1)S(1)} all-gather(bf16[128,272]{0,1:T(8,128)(2,1)S(1)} %get-tuple-element.55), channel_id=1, replica_groups=mesh['ctx'=8,'wa'=4] {'wa'}, dimensions={1}, use_global_device_ids=true | all-gather | bytes 348160 | tf_op jit(solution)/shard_map/all_gather | solution.py:181
  199.2 3.2 convolution_add_fusion
  202.4 1.6 fusion.122
  204.8 1.5 convolution_convert_fusion.1
  206.4 34.9 %all-reduce.8.cloned.1.call-done = bf16[128,1088]{0,1:T(8,128)(2,1)} async-done(((bf16[128,1088]{0,1:T(8,128)(2,1)}), bf16[128,1088]{0,1:T(8,128)(2,1)}) %all-reduce.8.cloned.1.call-update) | async-done | bytes 278544 | tf_op jit(solution)/shard_map/psum | solution.py:201
  241.3 2.1 fusion.59
  243.4 2.3 fusion.118
  245.6 0.8 copy-done.8
  246.5 1.1 convolution_convert_fusion.2
  248.2 19.8 %reduce-scatter.18.cloned.1.call-done = bf16[32,1088]{1,0:T(8,128)(2,1)} async-done(((bf16[128,1088]{1,0:T(8,128)(2,1)}), bf16[32,1088]{1,0:T(8,128)(2,1)}) %reduce-scatter.18.cloned.1.call-update) | async-done | bytes 69648 | tf_op jit(solution)/shard_map/reduce_scatter | solution.py:100
  268.0 1.4 compare_and_fusion
  269.4 0.8 reshape.638
  270.2 0.8 reshape.640
  271.1 1.8 reshape.643
  272.8 65.3 %all-gather.1 = bf16[32,32,17]{1,2,0:T(8,128)(2,1)S(1)} all-gather(bf16[1,32,17]{1,2,0:T(8,128)(2,1)S(1)} %bitcast.101), channel_id=1, replica_groups=mesh['ctx'=8,'wa'=4] {'ctx','wa'}, dimensions={0}, use_global_device_ids=true | all-gather | bytes 35904 | tf_op jit(solution)/shard_map/all_gather | solution.py:253
  338.1 67.5 %all-gather = bf16[32,32,17]{1,2,0:T(8,128)(2,1)S(1)} all-gather(bf16[1,32,17]{1,2,0:T(8,128)(2,1)S(1)} %bitcast.97), channel_id=1, replica_groups=mesh['ctx'=8,'wa'=4] {'ctx','wa'}, dimensions={0}, use_global_device_ids=true | all-gather | bytes 35904 | tf_op jit(solution)/shard_map/all_gather | solution.py:252
  405.9 1.8 convolution_convert_fusion.3
  407.8 4.3 copy.73
  412.1 3.5 fusion.65
  416.2 4.3 fusion.13
  420.7 65.1 %all-gather.3 = bf16[32,32,17]{1,2,0:T(8,128)(2,1)S(1)} all-gather(bf16[1,32,17]{1,2,0:T(8,128)(2,1)S(1)} %bitcast.102), channel_id=1, replica_groups=mesh['ctx'=8,'wa'=4] {'ctx','wa'}, dimensions={0}, use_global_device_ids=true | all-gather | bytes 35904 | tf_op jit(solution)/shard_map/all_gather | solution.py:255
  485.9 66.9 %all-gather.2 = bf16[32,32,17]{1,2,0:T(8,128)(2,1)S(1)} all-gather(bf16[1,32,17]{1,2,0:T(8,128)(2,1)S(1)} %copy.78), channel_id=1, replica_groups=mesh['ctx'=8,'wa'=4] {'ctx','wa'}, dimensions={0}, use_global_device_ids=true | all-gather | bytes 35904 | tf_op jit(solution)/shard_map/all_gather | solution.py:254
  553.1 4.3 copy.76
  557.4 3.0 fusion.15
  560.5 4.3 fusion.12
  565.2 0.8 concatenate.18
  566.0 17.8 %all_gather.48 = bf16[128,3264]{1,0:T(8,128)(2,1)S(1)} all-gather(bf16[32,3264]{1,0:T(8,128)(2,1)} %concatenate.18), channel_id=1, replica_groups=mesh['ctx'=8,'wa'=4] {'wa'}, dimensions={0}, use_global_device_ids=true | all-gather | bytes 1044480 | tf_op jit(solution)/shard_map/all_gather | solution.py:108
  583.8 3.4 fusion.113
  587.3 2.7 fusion.74
  590.1 4.4 fusion.71
  594.5 4.2 fusion.117
  598.8 1.4 dynamic_slice.18
  601.6 1.7 add_convert_fusion.1
  603.3 2.1 convolution_convert_fusion.5
  605.4 13.8 %all_gather.49 = bf16[128,1088]{0,1:T(8,128)(2,1)S(1)} all-gather(bf16[128,272]{0,1:T(8,128)(2,1)S(1)} %convolution_convert_fusion.5), channel_id=1, replica_groups=mesh['ctx'=8,'wa'=4] {'wa'}, dimensions={1}, use_global_device_ids=true | all-gather | bytes 348160 | tf_op jit(solution)/shard_map/all_gather | solution.py:298
  620.1 23.7 %all-reduce.4 = (f32[8,1088]{1,0:T(8,128)S(1)}, f32[1088]{0:T(1024)}) all-reduce(f32[8,1088]{1,0:T(8,128)S(1)} %stack.35, f32[1088]{0:T(1024)S(1)} %copy-done.47), channel_id=1, replica_groups=mesh['ctx'=8,'wa'=4] {'ctx'}, use_global_device_ids=true, to_apply=%region_23.24 | all-reduce | flops 9792 | bytes 78336 | tf_op jit(solution)/shard_map/psum | solution.py:324
  644.6 2.2 fusion.45
  646.8 13.7 %all-reduce.10.cloned.1.call-done = f32[272,3264]{1,0:T(8,128)} async-done(((f32[272,3264]{1,0:T(8,128)}), f32[272,3264]{1,0:T(8,128)}) %all-reduce.10.cloned.1.call-update) | async-done | bytes 3551248
  660.5 2.1 constant_dynamic-slice_fusion
  662.6 40.0 %reduce-scatter.20.cloned.1.call-done = f32[272,136]{0,1:T(8,128)} async-done(((f32[272,1088]{0,1:T(8,128)}), f32[272,136]{0,1:T(8,128)}) %reduce-scatter.20.cloned.1.call-update) | async-done | bytes 147984
  702.6 58.8 %reduce-scatter.22.cloned.1.call-done = f32[1088,136]{0,1:T(8,128)} async-done(((f32[1088,1088]{0,1:T(8,128)}), f32[1088,136]{0,1:T(8,128)}) %reduce-scatter.22.cloned.1.call-update) | async-done | bytes 591888
  761.4 58.7 %reduce-scatter.24.cloned.1.call-done = f32[1088,136]{0,1:T(8,128)} async-done(((f32[1088,1088]{0,1:T(8,128)}), f32[1088,136]{0,1:T(8,128)}) %reduce-scatter.24.cloned.1.call-update) | async-done | bytes 591888
  (187 shorter events, 10.1 us)
Async XLA Ops:
  7.2 195.2 %copy-start = (bf16[1088,1088]{1,0:T(8,128)(2,1)S(1)}, bf16[1088,1088]{1,0:T(8,128)(2,1)}, u32[]{:S(2)}) copy-start(bf16[1088,1088]{1,0:T(8,128)(2,1)} %param.31) | copy-start | bytes 7102468
  7.2 35.6 %reduce-scatter.14.cloned.1.call-start = ((), (), s32[]{:S(2)}) async-start(), calls=%async_computation.6 | async-start | bytes 1064960 | tf_op jit(solution)/shard_map/reduce_scatter | solution.py:100
  10.1 0.6 copy-start.41
  10.1 0.6 copy-start.43
  10.7 5.1 copy-start.45
  10.7 5.2 copy-start.46
  11.7 0.8 copy-start.15
  12.5 32.8 %copy-start.6 = (bf16[128,1088]{0,1:T(8,128)(2,1)S(1)}, bf16[128,1088]{0,1:T(8,128)(2,1)}, u32[]{:S(2)}) copy-start(bf16[128,1088]{0,1:T(8,128)(2,1)} %param.17) | copy-start | bytes 835588
  12.5 34.5 %copy-start.1 = (s32[8,2]{0,1:T(2,128)S(1)}, s32[8,2]{0,1:T(2,128)}, u32[]{:S(2)}) copy-start(s32[8,2]{0,1:T(2,128)} %param.18) | copy-start | bytes 196
  15.7 86.7 %all-gather.9.cloned.1.call-start = ((), (), s32[]{:S(2)}) async-start(), calls=%async_computation.7 | async-start | bytes 2433024 | tf_op jit(solution)/shard_map/all_gather | solution.py:122
  44.5 17.6 %copy-start.18 = (bf16[32,1088]{1,0:T(8,128)(2,1)}, bf16[32,1088]{1,0:T(8,128)(2,1)S(1)}, u32[]{:S(2)}) copy-start(bf16[32,1088]{1,0:T(8,128)(2,1)S(1)} %get-tuple-element.40) | copy-start | bytes 208900
  44.5 116.6 %all-gather.11.cloned.1.call-start = ((), (), s32[]{:S(2)}) async-start(), calls=%async_computation.8 | async-start | bytes 2433024 | tf_op jit(solution)/shard_map/all_gather | solution.py:123
  45.3 196.0 %all-reduce.8.cloned.1.call-start = ((), (), s32[]{:S(2)}) async-start(), calls=%async_computation.10 | async-start | bytes 557056 | tf_op jit(solution)/shard_map/psum | solution.py:201
  47.0 9.7 %copy-start.2 = (s32[1024]{0:T(1024)S(1)}, s32[1024]{0:T(1024)}, u32[]{:S(2)}) copy-start(s32[1024]{0:T(1024)} %param.19) | copy-start | bytes 12292
  56.7 5.3 copy-start.28
  61.2 45.5 %copy-start.29 = (s32[1024]{0:T(1024)}, s32[1024]{0:T(1024)S(1)}, u32[]{:S(2)}) copy-start(s32[1024]{0:T(1024)S(1)} %gather_fusion.1) | copy-start | bytes 12292
  61.9 44.8 %copy-start.48 = (s32[32]{0:T(128)}, s32[32]{0:T(128)S(1)}, u32[]{:S(2)}) copy-start(s32[32]{0:T(128)S(1)} %gather_fusion.3) | copy-start | bytes 388
  62.0 44.7 %copy-start.49 = (s32[32]{0:T(128)}, s32[32]{0:T(128)S(1)}, u32[]{:S(2)}) copy-start(s32[32]{0:T(128)S(1)} %fusion.95) | copy-start | bytes 388
  109.1 1.4 copy-start.4
  165.4 17.5 %copy-start.11 = (bf16[1088,272]{0,1:T(8,128)(2,1)S(1)}, bf16[1088,272]{0,1:T(8,128)(2,1)}, u32[]{:S(2)}) copy-start(bf16[1088,272]{0,1:T(8,128)(2,1)} %param.25) | copy-start | bytes 1775620
  168.6 30.6 %copy-start.26 = (f32[1088]{0:T(1024)S(1)}, f32[1088]{0:T(1024)}, u32[]{:S(2)}) copy-start(f32[1088]{0:T(1024)} %param.27) | copy-start | bytes 13060
  168.6 30.6 %copy-start.30 = (f32[1088]{0:T(1024)S(1)}, f32[1088]{0:T(1024)}, u32[]{:S(2)}) copy-start(f32[1088]{0:T(1024)} %param.28) | copy-start | bytes 13060
  168.8 30.4 %copy-start.21 = (bf16[32,1088]{1,0:T(8,128)(2,1)}, bf16[32,1088]{1,0:T(8,128)(2,1)S(1)}, u32[]{:S(2)}) copy-start(bf16[32,1088]{1,0:T(8,128)(2,1)S(1)} %convert_element_type.141) | copy-start | bytes 208900
  182.9 16.3 %copy-start.9 = (bf16[128,1088]{1,0:T(8,128)(2,1)}, bf16[128,1088]{1,0:T(8,128)(2,1)S(1)}, u32[]{:S(2)}) copy-start(bf16[128,1088]{1,0:T(8,128)(2,1)S(1)} %all_gather.40) | copy-start | bytes 835588
  184.9 17.5 %copy-start.16 = (bf16[128,1088]{0,1:T(8,128)(2,1)S(1)}, bf16[128,1088]{0,1:T(8,128)(2,1)}, u32[]{:S(2)}) copy-start(bf16[128,1088]{0,1:T(8,128)(2,1)} %param.33) | copy-start | bytes 835588
  199.0 44.4 %copy-start.3 = (bf16[128,1088]{0,1:T(8,128)(2,1)}, bf16[128,1088]{0,1:T(8,128)(2,1)S(1)}, u32[]{:S(2)}) copy-start(bf16[128,1088]{0,1:T(8,128)(2,1)S(1)} %all_gather.41) | copy-start | bytes 835588
  199.2 4.9 copy-start.37
  199.2 4.9 copy-start.39
  202.4 203.5 %copy-start.5 = (f32[128,1088]{0,1:T(8,128)}, f32[128,1088]{0,1:T(8,128)S(1)}, u32[]{:S(2)}) copy-start(f32[128,1088]{0,1:T(8,128)S(1)} %convolution_add_fusion) | copy-start | bytes 1671172
  202.4 2.3 copy-start.10
  204.0 0.7 copy-start.17
  206.3 63.1 %copy-start.20 = (bf16[32,1088]{1,0:T(8,128)(2,1)S(1)}, bf16[32,1088]{1,0:T(8,128)(2,1)}, u32[]{:S(2)}) copy-start(bf16[32,1088]{1,0:T(8,128)(2,1)} %get-tuple-element.42) | copy-start | bytes 208900
  206.3 64.0 %copy-start.19 = (bf16[32,1088]{1,0:T(8,128)(2,1)S(1)}, bf16[32,1088]{1,0:T(8,128)(2,1)}, u32[]{:S(2)}) copy-start(bf16[32,1088]{1,0:T(8,128)(2,1)} %get-tuple-element.41) | copy-start | bytes 208900
  206.3 61.6 %reduce-scatter.18.cloned.1.call-start = ((), (), s32[]{:S(2)}) async-start(), calls=%async_computation.11 | async-start | bytes 368640 | tf_op jit(solution)/shard_map/reduce_scatter | solution.py:100
  241.3 5.2 copy-start.12
  245.6 0.8 copy-start.8
  247.5 160.3 %all-gather.13.cloned.1.call-start = ((), (), s32[]{:S(2)}) async-start(), calls=%async_computation.12 | async-start | bytes 2433024 | tf_op jit(solution)/shard_map/all_gather | solution.py:250
  248.1 305.0 %all-gather.15.cloned.1.call-start = ((), (), s32[]{:S(2)}) async-start(), calls=%async_computation.13 | async-start | bytes 2433024 | tf_op jit(solution)/shard_map/all_gather | solution.py:251
  268.0 333.7 %reduce-scatter.16.cloned.1.call-start = ((), (), s32[]{:S(2)}) async-start(), calls=%async_computation.9 | async-start | bytes 348160 | tf_op jit(solution)/shard_map/reduce_scatter | solution.py:189
  407.7 4.4 copy-start.22
  407.7 252.8 %all-reduce.10.cloned.1.call-start = ((), (), s32[]{:S(2)}) async-start(), calls=%async_computation.14 | async-start | bytes 7241728
  412.1 3.5 copy-start.24
  412.1 3.6 copy-start.14
  553.1 4.3 copy-start.36
  557.4 3.1 copy-start.25
  587.2 2.8 copy-start.31
  587.2 2.8 copy-start.38
  587.2 2.8 copy-start.40
  587.2 115.4 %reduce-scatter.20.cloned.1.call-start = ((), (), s32[]{:S(2)}) async-start(), calls=%async_computation.15 | async-start | bytes 1880064
  590.0 171.4 %reduce-scatter.22.cloned.1.call-start = ((), (), s32[]{:S(2)}) async-start(), calls=%async_computation.16 | async-start | bytes 5640192
  594.4 225.7 %reduce-scatter.24.cloned.1.call-start = ((), (), s32[]{:S(2)}) async-start(), calls=%async_computation.17 | async-start | bytes 5640192
  598.7 1.5 copy-start.50
  598.7 2.8 copy-start.33
  598.7 2.8 copy-start.32
  598.7 2.8 copy-start.35
  598.7 2.8 copy-start.34
  598.8 2.9 copy-start.23
  598.8 20.5 %copy-start.27 = (f32[1088]{0:T(1024)S(1)}, f32[1088]{0:T(1024)}, u32[]{:S(2)}) copy-start(f32[1088]{0:T(1024)} %param.20) | copy-start | bytes 13060
  598.8 20.5 %copy-start.42 = (f32[128]{0:T(128)S(1)}, f32[128]{0:T(128)}, u32[]{:S(2)}) copy-start(f32[128]{0:T(128)} %copy-done.41) | copy-start | bytes 1540
  598.8 20.5 %copy-start.44 = (f32[128]{0:T(128)S(1)}, f32[128]{0:T(128)}, u32[]{:S(2)}) copy-start(f32[128]{0:T(128)} %copy-done.43) | copy-start | bytes 1540
  601.6 17.7 %copy-start.7 = (bf16[128,1088]{0,1:T(8,128)(2,1)S(1)}, bf16[128,1088]{0,1:T(8,128)(2,1)}, u32[]{:S(2)}) copy-start(bf16[128,1088]{0,1:T(8,128)(2,1)} %param.17) | copy-start | bytes 835588
  603.3 16.8 %copy-start.47 = (f32[1088]{0:T(1024)S(1)}, f32[1088]{0:T(1024)}, u32[]{:S(2)}) copy-start(f32[1088]{0:T(1024)} %get-tuple-element.57) | copy-start | bytes 13060
  619.3 0.7 copy-start.13
Sparse Core Ops, SparseCore 0:
  15.9 26.9 reduce-scatter.13
  46.2 56.2 all-gather.8
  105.3 55.8 all-gather.10
  206.4 34.7 all-reduce.7
  247.7 20.2 reduce-scatter.17
  270.6 55.5 all-gather.12
  329.0 55.9 all-gather.14
  407.8 17.8 reduce-scatter.15
  587.3 73.1 all-reduce.9
  664.2 38.3 reduce-scatter.19
  706.7 54.7 reduce-scatter.21
  765.3 54.7 reduce-scatter.23
where the time goes:
time: 828 us; the launch traced here: 827 us
  blocking collectives  348 us (42%)
  waiting for transfers between devices  344 us (42%)
  matrix products  51.8 us (6%)
  local copies, waits for them, and re-layouts  50.5 us (6%)
  other arithmetic  15.7 us (2%)
  between operations  15.7 us (2%)
    unnamed x16, waiting for transfers between devices  173 us
    all_gather x1, blocking collectives, body(): log_high = lax.all_gather(pieces[2], ('ctx', 'wa'), axis=0, tiled=True)  67.5 us
    all_gather x1, blocking collectives, body(): delta_high = lax.all_gather(pieces[4], ('ctx', 'wa'), axis=0, tiled=True)  66.9 us
    all_gather x1, blocking collectives, body(): log_low = lax.all_gather(pieces[3], ('ctx', 'wa'), axis=0, tiled=True)  65.3 us
    all_gather x1, blocking collectives, body(): delta_low = lax.all_gather(pieces[5], ('ctx', 'wa'), axis=0, tiled=True)  65.1 us
    all_gather x1, waiting for transfers between devices, fold_keys(): lax.all_gather(val_rows, ('ctx', 'wa'), axis=0, tiled=True)  50.1 us
    reduce_scatter x2, waiting for transfers between devices, row_sums(): lax.psum_scatter(term_fn(jnp.int32(0), lax.axis_size('wa') * rows_here).a...  46.7 us
    all_gather x1, waiting for transfers between devices, fold_keys(): lax.all_gather(key_rows, ('ctx', 'wa'), axis=0, tiled=True)  40.2 us
  transfers between devices with their start and end apart: 12, of which 9 were waited for; matrix products, arithmetic and copies ran while one was open for 10% of the time, Pallas kernels for 0%

commit v1 on v0

--- a/solution.py
+++ b/solution.py
@@ -116,10 +116,24 @@
     val_rows = qkv_own[:, 2 * model_width :]
 
     def fold_keys(fold_fn, init):
+
+        def map_targets(net_axis, mat):
+            s_next, everything = (lax.axis_size(net_axis), lax.axis_index(net_axis))
+            opened, block_now = (mat, 1)
+            while block_now < s_next:
+                z = lax.ppermute(
+                    opened, axis_name=net_axis, perm=[(j, j ^ block_now) for j in range(s_next)]
+                )
+                local_now = jnp.concatenate([opened, z], axis=0)
+                current_arr = jnp.concatenate([z, opened], axis=0)
+                opened = jnp.where(everything & block_now == 0, local_now, current_arr)
+                block_now = 2 * block_now
+            return opened
+
         return fold_fn(
             init,
             (
-                lax.all_gather(key_rows, ("ctx", "wa"), axis=0, tiled=True),
+                map_targets(("ctx", "wa"), key_rows),
                 lax.all_gather(val_rows, ("ctx", "wa"), axis=0, tiled=True),
             ),
             jnp.int32(0),

time: 828 us -> 790 us (0.954)
  waiting for transfers between devices: 344 us -> 292 us
  other arithmetic: 15.7 us -> 25.9 us
    all_gather x1, waiting for transfers between devices: 50.1 us -> 0.02 us  [fold_keys(): lax.all_gather(val_rows, ('ctx', 'wa'), axis=0, tiled=True)]
    all_gather x1 -> x0, waiting for transfers between devices: 40.2 us -> none  [fold_keys(): lax.all_gather(key_rows, ('ctx', 'wa'), axis=0, tiled=True)]
    ppermute x0 -> x5, waiting for transfers between devices: none -> 35.8 us  [map_targets(): lax.ppermute(opened, axis_name=net_axis, perm=[(j, j ^ block_now) for j i...]
    unnamed x16 -> x15, waiting for transfers between devices: 173 us -> 173 us
  transfers between devices with their start and end apart: 12 -> 16, of which waited for: 9 -> 11; matrix products, arithmetic and copies ran while one was open for 10% -> 12% of each run, Pallas kernels for 0% -> 0%
where the time goes in v1:
time: 790 us; the launch traced here: 788 us
  blocking collectives  349 us (44%)
  waiting for transfers between devices  292 us (37%)
  local copies, waits for them, and re-layouts  54.7 us (7%)
  matrix products  47 us (6%)
  other arithmetic  25.9 us (3%)
  between operations  15.6 us (2%)
    unnamed x15, waiting for transfers between devices  173 us
    all_gather x1, blocking collectives, body(): log_high = lax.all_gather(pieces[2], ('ctx', 'wa'), axis=0, tiled=True)  67.7 us
    all_gather x1, blocking collectives, body(): delta_high = lax.all_gather(pieces[4], ('ctx', 'wa'), axis=0, tiled=True)  67.3 us
    all_gather x1, blocking collectives, body(): log_low = lax.all_gather(pieces[3], ('ctx', 'wa'), axis=0, tiled=True)  65.3 us
    all_gather x1, blocking collectives, body(): delta_low = lax.all_gather(pieces[5], ('ctx', 'wa'), axis=0, tiled=True)  64.9 us
    reduce_scatter x2, waiting for transfers between devices, row_sums(): lax.psum_scatter(term_fn(jnp.int32(0), lax.axis_size('wa') * rows_here).a...  46.6 us
    psum x1, waiting for transfers between devices, body(): lax.psum(contract_cols(hidden_grad_b, up_weight).astype(jnp.bfloat16), 'wa')  36.3 us
    ppermute x5, waiting for transfers between devices, map_targets(): lax.ppermute(opened, axis_name=net_axis, perm=[(j, j ^ block_now) for j i...  35.8 us
  transfers between devices with their start and end apart: 16, of which 11 were waited for; matrix products, arithmetic and copies ran while one was open for 12% of the time, Pallas kernels for 0%

profile of v1, /device:TPU:0, one launch (start us, length us, event | category | flops | bytes accessed | tf_op | source)
XLA Modules:
  0.0 788.4 jit_solution(4084652596925273678)
XLA Ops:
  7.2 1.3 convert_reduce_fusion.5
  10.1 1.0 subtract_multiply_fusion
  12.0 3.2 convolution_convert_fusion
  15.4 26.9 %reduce-scatter.14.cloned.1.call-done = bf16[32,3264]{1,0:T(8,128)(2,1)} async-done(((bf16[128,3264]{1,0:T(8,128)(2,1)}), bf16[32,3264]{1,0:T(8,128)(2,1)}) %reduce-scatter.14.cloned.1.call-update) | async-done | bytes 208912 | tf_op jit(solution)/shard_map/reduce_scatter | solution.py:100
  44.0 4.3 collective-permute-done
  49.2 6.8 collective-permute-done.1
  57.7 1.3 dynamic_slice.17
  59.1 8.8 %gather_fusion = s32[1024]{0:T(1024)S(1)} fusion(s32[8,2]{0,1:T(2,128)S(1)} %copy-done.2, s32[1024]{0:T(1024)S(1)} %bitcast.88), kind=kCustom, calls=%fused_computation | custom fusion | bytes 16384 | tf_op jit(solution)/shard_map/gather | solution.py:59
  68.5 1.3 maximum_select_fusion.3
  69.8 1.0 copy.85
  70.8 1.4 collective-permute-start.3
  72.3 1.3 gather_fusion.2
  74.9 5.0 gather_fusion.1
  79.9 6.3 collective-permute-done.3
  86.1 2.2 copy.86
  88.3 2.7 maximum_select_fusion.1
  91.0 2.4 copy.88
  93.4 1.6 collective-permute-start.4
  97.8 1.4 maximum_select_fusion.8
  99.6 1.6 maximum_select_fusion.2
  101.2 18.5 %collective-permute-done.4 = bf16[512,1088]{0,1:T(8,128)(2,1)} collective-permute-done((bf16[512,1088]{0,1:T(8,128)(2,1)}, bf16[512,1088]{0,1:T(8,128)(2,1)}, u32[]{:S(2)}, u32[]{:S(2)}) %collective-permute-start.4) | collective-permute-done | bytes 1114144 | tf_op jit(solution)/shard_map/ppermute | solution.py:124
  119.7 2.7 select_reduce_fusion
  122.4 1.4 copy-done.17
  124.5 4.2 copy.90
  128.8 3.2 fusion.11
  132.2 14.0 %all_gather.35 = bf16[128,1088]{1,0:T(8,128)(2,1)S(1)} all-gather(bf16[32,1088]{1,0:T(8,128)(2,1)S(1)} %convert_element_type.141), channel_id=1, replica_groups=mesh['ctx'=8,'wa'=4] {'wa'}, dimensions={0}, use_global_device_ids=true | all-gather | bytes 348160 | tf_op jit(solution)/shard_map/all_gather | solution.py:108
  146.2 2.0 fusion.123
  148.3 14.2 %all_gather.36 = bf16[128,1088]{0,1:T(8,128)(2,1)S(1)} all-gather(bf16[128,272]{0,1:T(8,128)(2,1)S(1)} %get-tuple-element.55), channel_id=1, replica_groups=mesh['ctx'=8,'wa'=4] {'wa'}, dimensions={1}, use_global_device_ids=true | all-gather | bytes 348160 | tf_op jit(solution)/shard_map/all_gather | solution.py:195
  162.8 3.2 convolution_add_fusion
  166.0 1.6 fusion.124
  168.3 1.5 convolution_convert_fusion.1
  169.9 36.3 %all-reduce.8.cloned.1.call-done = bf16[128,1088]{0,1:T(8,128)(2,1)} async-done(((bf16[128,1088]{0,1:T(8,128)(2,1)}), bf16[128,1088]{0,1:T(8,128)(2,1)}) %all-reduce.8.cloned.1.call-update) | async-done | bytes 278544 | tf_op jit(solution)/shard_map/psum | solution.py:215
  206.2 2.1 fusion.59
  208.3 2.3 fusion.120
  211.4 1.1 convolution_convert_fusion.2
  213.1 19.8 %reduce-scatter.18.cloned.1.call-done = bf16[32,1088]{1,0:T(8,128)(2,1)} async-done(((bf16[128,1088]{1,0:T(8,128)(2,1)}), bf16[32,1088]{1,0:T(8,128)(2,1)}) %reduce-scatter.18.cloned.1.call-update) | async-done | bytes 69648 | tf_op jit(solution)/shard_map/reduce_scatter | solution.py:100
  232.9 1.4 compare_and_fusion
  236.0 65.3 %all-gather.1 = bf16[32,32,17]{1,2,0:T(8,128)(2,1)S(1)} all-gather(bf16[1,32,17]{1,2,0:T(8,128)(2,1)S(1)} %bitcast.104), channel_id=1, replica_groups=mesh['ctx'=8,'wa'=4] {'ctx','wa'}, dimensions={0}, use_global_device_ids=true | all-gather | bytes 35904 | tf_op jit(solution)/shard_map/all_gather | solution.py:267
  301.3 67.7 %all-gather = bf16[32,32,17]{1,2,0:T(8,128)(2,1)S(1)} all-gather(bf16[1,32,17]{1,2,0:T(8,128)(2,1)S(1)} %bitcast.100), channel_id=1, replica_groups=mesh['ctx'=8,'wa'=4] {'ctx','wa'}, dimensions={0}, use_global_device_ids=true | all-gather | bytes 35904 | tf_op jit(solution)/shard_map/all_gather | solution.py:266
  369.9 1.0 reshape.656
  370.9 1.8 convolution_convert_fusion.3
  372.8 3.0 copy.95
  375.8 1.8 fusion.66
  378.2 5.3 fusion.13
  383.8 64.9 %all-gather.3 = bf16[32,32,17]{1,2,0:T(8,128)(2,1)S(1)} all-gather(bf16[1,32,17]{1,2,0:T(8,128)(2,1)S(1)} %bitcast.105), channel_id=1, replica_groups=mesh['ctx'=8,'wa'=4] {'ctx','wa'}, dimensions={0}, use_global_device_ids=true | all-gather | bytes 35904 | tf_op jit(solution)/shard_map/all_gather | solution.py:269
  448.8 67.3 %all-gather.2 = bf16[32,32,17]{1,2,0:T(8,128)(2,1)S(1)} all-gather(bf16[1,32,17]{1,2,0:T(8,128)(2,1)S(1)} %copy.100), channel_id=1, replica_groups=mesh['ctx'=8,'wa'=4] {'ctx','wa'}, dimensions={0}, use_global_device_ids=true | all-gather | bytes 35904 | tf_op jit(solution)/shard_map/all_gather | solution.py:268
  516.3 4.2 copy.98
  520.6 3.1 fusion.15
  523.7 3.7 fusion.12
  527.9 17.6 %all_gather.43 = bf16[128,3264]{1,0:T(8,128)(2,1)S(1)} all-gather(bf16[32,3264]{1,0:T(8,128)(2,1)S(1)} %concatenate.109), channel_id=1, replica_groups=mesh['ctx'=8,'wa'=4] {'wa'}, dimensions={0}, use_global_device_ids=true | all-gather | bytes 1044480 | tf_op jit(solution)/shard_map/all_gather | solution.py:108
  545.5 3.5 fusion.115
  550.0 2.5 fusion.74
  552.6 3.2 fusion.71
  556.9 3.1 fusion.119
  562.4 1.6 add_convert_fusion.1
  564.7 14.0 %all_gather.44 = bf16[128,1088]{0,1:T(8,128)(2,1)S(1)} all-gather(bf16[128,272]{0,1:T(8,128)(2,1)S(1)} %convolution_convert_fusion.5), channel_id=1, replica_groups=mesh['ctx'=8,'wa'=4] {'wa'}, dimensions={1}, use_global_device_ids=true | all-gather | bytes 348160 | tf_op jit(solution)/shard_map/all_gather | solution.py:312
  578.7 1.5 fusion.60
  580.5 23.9 %all-reduce.4 = (f32[8,1088]{1,0:T(8,128)S(1)}, f32[1088]{0:T(1024)}) all-reduce(f32[8,1088]{1,0:T(8,128)S(1)} %stack.35, f32[1088]{0:T(1024)S(1)} %copy-done.64), channel_id=1, replica_groups=mesh['ctx'=8,'wa'=4] {'ctx'}, use_global_device_ids=true, to_apply=%region_23.24 | all-reduce | flops 9792 | bytes 78336 | tf_op jit(solution)/shard_map/psum | solution.py:338
  605.1 2.3 fusion.45
  607.5 14.6 %all-reduce.10.cloned.1.call-done = f32[272,3264]{1,0:T(8,128)} async-done(((f32[272,3264]{1,0:T(8,128)}), f32[272,3264]{1,0:T(8,128)}) %all-reduce.10.cloned.1.call-update) | async-done | bytes 3551248
  622.1 2.1 constant_dynamic-slice_fusion
  624.2 40.2 %reduce-scatter.20.cloned.1.call-done = f32[272,136]{0,1:T(8,128)} async-done(((f32[272,1088]{0,1:T(8,128)}), f32[272,136]{0,1:T(8,128)}) %reduce-scatter.20.cloned.1.call-update) | async-done | bytes 147984
  664.4 58.7 %reduce-scatter.22.cloned.1.call-done = f32[1088,136]{0,1:T(8,128)} async-done(((f32[1088,1088]{0,1:T(8,128)}), f32[1088,136]{0,1:T(8,128)}) %reduce-scatter.22.cloned.1.call-update) | async-done | bytes 591888
  723.0 58.8 %reduce-scatter.24.cloned.1.call-done = f32[1088,136]{0,1:T(8,128)} async-done(((f32[1088,1088]{0,1:T(8,128)}), f32[1088,136]{0,1:T(8,128)}) %reduce-scatter.24.cloned.1.call-update) | async-done | bytes 591888
  (242 shorter events, 24.9 us)
Async XLA Ops:
  7.2 158.8 %copy-start = (bf16[1088,1088]{1,0:T(8,128)(2,1)S(1)}, bf16[1088,1088]{1,0:T(8,128)(2,1)}, u32[]{:S(2)}) copy-start(bf16[1088,1088]{1,0:T(8,128)(2,1)} %param.31) | copy-start | bytes 7102468
  7.2 35.1 %reduce-scatter.14.cloned.1.call-start = ((), (), s32[]{:S(2)}) async-start(), calls=%async_computation.6 | async-start | bytes 1064960 | tf_op jit(solution)/shard_map/reduce_scatter | solution.py:100
  10.1 5.1 copy-start.40
  10.1 5.1 copy-start.57
  10.1 5.1 copy-start.59
  10.1 5.2 copy-start.62
  10.1 5.2 copy-start.63
  12.0 44.9 %copy-start.9 = (bf16[128,1088]{0,1:T(8,128)(2,1)S(1)}, bf16[128,1088]{0,1:T(8,128)(2,1)}, u32[]{:S(2)}) copy-start(bf16[128,1088]{0,1:T(8,128)(2,1)} %param.17) | copy-start | bytes 835588
  15.2 43.9 %copy-start.2 = (s32[8,2]{0,1:T(2,128)S(1)}, s32[8,2]{0,1:T(2,128)}, u32[]{:S(2)}) copy-start(s32[8,2]{0,1:T(2,128)} %param.18) | copy-start | bytes 196
  15.2 109.3 %all-gather.8.cloned.1.call-start = ((), (), s32[]{:S(2)}) async-start(), calls=%async_computation.7 | async-start | bytes 2433024 | tf_op jit(solution)/shard_map/all_gather | solution.py:137
  43.9 5.3 copy-start.27
  43.9 4.4 collective-permute-start
  44.0 162.2 %all-reduce.8.cloned.1.call-start = ((), (), s32[]{:S(2)}) async-start(), calls=%async_computation.9 | async-start | bytes 557056 | tf_op jit(solution)/shard_map/psum | solution.py:215
  48.3 7.7 collective-permute-start.1
  56.7 11.2 %copy-start.19 = (bf16[128,1088]{1,0:T(8,128)(2,1)}, bf16[128,1088]{1,0:T(8,128)(2,1)S(1)}, u32[]{:S(2)}) copy-start(bf16[128,1088]{1,0:T(8,128)(2,1)S(1)} %maximum_select_fusion.7) | copy-start | bytes 835588
  56.7 11.8 %collective-permute-start.2 = (bf16[128,1088]{1,0:T(8,128)(2,1)S(1)}, bf16[128,1088]{1,0:T(8,128)(2,1)S(1)}, u32[]{:S(2)}, u32[]{:S(2)}) collective-permute-start(bf16[128,1088]{1,0:T(8,128)(2,1)S(1)} %maximum_select_fusion.7), channel_id=1, source_target_pairs={{0,4},{1,5},{2,6},{3,7},{4,0},{5,1},{6,2},{7,3},{8,12},{9,13},{10,... | collective-permute-start | bytes 835592 | tf_op jit(solution)/shard_map/ppermute | solution.py:124
  67.9 6.9 copy-start.3
  70.8 15.3 %collective-permute-start.3 = (bf16[256,1088]{0,1:T(8,128)(2,1)}, bf16[256,1088]{0,1:T(8,128)(2,1)}, u32[]{:S(2)}, u32[]{:S(2)}) collective-permute-start(bf16[256,1088]{0,1:T(8,128)(2,1)} %copy.85), channel_id=1, source_target_pairs={{0,8},{1,9},{2,10},{3,11},{4,12},{5,13},{6,14},{7,15},{8,0},{9,1},... | collective-permute-start | bytes 1671176 | tf_op jit(solution)/shard_map/ppermute | solution.py:124
  79.9 15.9 %copy-start.44 = (s32[1024]{0:T(1024)}, s32[1024]{0:T(1024)S(1)}, u32[]{:S(2)}) copy-start(s32[1024]{0:T(1024)S(1)} %gather_fusion.1) | copy-start | bytes 12292
  88.3 7.4 copy-start.43
  91.0 4.0 copy-start.67
  91.0 4.9 copy-start.25
  91.0 5.9 copy-start.31
  93.4 26.3 %collective-permute-start.4 = (bf16[512,1088]{0,1:T(8,128)(2,1)}, bf16[512,1088]{0,1:T(8,128)(2,1)}, u32[]{:S(2)}, u32[]{:S(2)}) collective-permute-start(bf16[512,1088]{0,1:T(8,128)(2,1)} %copy.88), channel_id=1, source_target_pairs={{0,16},{1,17},{2,18},{3,19},{4,20},{5,21},{6,22},{7,23},{8,24},{9,... | collective-permute-start | bytes 3342344 | tf_op jit(solution)/shard_map/ppermute | solution.py:124
  95.7 5.5 copy-start.65
  95.9 26.5 %copy-start.37 = (pred[32,1024]{1,0:T(8,128)(4,1)}, pred[32,1024]{1,0:T(8,128)(4,1)S(1)}, u32[]{:S(2)}) copy-start(pred[32,1024]{1,0:T(8,128)(4,1)S(1)} %compare_and_fusion.1) | copy-start | bytes 98308
  101.2 21.2 %copy-start.22 = (bf16[512,17,64]{0,2,1:T(8,128)(2,1)}, bf16[512,17,64]{0,2,1:T(8,128)(2,1)S(1)}, u32[]{:S(2)}) copy-start(bf16[512,17,64]{0,2,1:T(8,128)(2,1)S(1)} %maximum_select_fusion.2) | copy-start | bytes 3342340
  124.5 4.3 copy-start.38
  128.7 17.5 %copy-start.14 = (bf16[1088,272]{0,1:T(8,128)(2,1)S(1)}, bf16[1088,272]{0,1:T(8,128)(2,1)}, u32[]{:S(2)}) copy-start(bf16[1088,272]{0,1:T(8,128)(2,1)} %param.25) | copy-start | bytes 1775620
  128.7 17.5 %copy-start.61 = (f32[272]{0:T(512)S(1)}, f32[272]{0:T(512)}, u32[]{:S(2)}) copy-start(f32[272]{0:T(512)} %dynamic_slice.17) | copy-start | bytes 3268
  131.9 30.8 %copy-start.36 = (f32[1088]{0:T(1024)S(1)}, f32[1088]{0:T(1024)}, u32[]{:S(2)}) copy-start(f32[1088]{0:T(1024)} %param.27) | copy-start | bytes 13060
  131.9 30.8 %copy-start.45 = (f32[1088]{0:T(1024)S(1)}, f32[1088]{0:T(1024)}, u32[]{:S(2)}) copy-start(f32[1088]{0:T(1024)} %param.28) | copy-start | bytes 13060
  132.0 30.8 %copy-start.56 = (f32[1088]{0:T(1024)S(1)}, f32[1088]{0:T(1024)}, u32[]{:S(2)}) copy-start(f32[1088]{0:T(1024)} %param.30) | copy-start | bytes 13060
  132.2 16.1 %copy-start.29 = (bf16[32,1088]{1,0:T(8,128)(2,1)}, bf16[32,1088]{1,0:T(8,128)(2,1)S(1)}, u32[]{:S(2)}) copy-start(bf16[32,1088]{1,0:T(8,128)(2,1)S(1)} %convert_element_type.141) | copy-start | bytes 208900
  146.2 16.5 %copy-start.11 = (bf16[128,1088]{1,0:T(8,128)(2,1)}, bf16[128,1088]{1,0:T(8,128)(2,1)S(1)}, u32[]{:S(2)}) copy-start(bf16[128,1088]{1,0:T(8,128)(2,1)S(1)} %all_gather.35) | copy-start | bytes 835588
  148.3 17.7 %copy-start.20 = (bf16[128,1088]{0,1:T(8,128)(2,1)S(1)}, bf16[128,1088]{0,1:T(8,128)(2,1)}, u32[]{:S(2)}) copy-start(bf16[128,1088]{0,1:T(8,128)(2,1)} %param.33) | copy-start | bytes 835588
  162.5 45.8 %copy-start.4 = (bf16[128,1088]{0,1:T(8,128)(2,1)}, bf16[128,1088]{0,1:T(8,128)(2,1)S(1)}, u32[]{:S(2)}) copy-start(bf16[128,1088]{0,1:T(8,128)(2,1)S(1)} %all_gather.36) | copy-start | bytes 835588
  162.7 4.9 copy-start.52
  162.7 4.9 copy-start.54
  166.0 205.0 %copy-start.6 = (f32[128,1088]{0,1:T(8,128)}, f32[128,1088]{0,1:T(8,128)S(1)}, u32[]{:S(2)}) copy-start(f32[128,1088]{0,1:T(8,128)S(1)} %convolution_add_fusion) | copy-start | bytes 1671172
  169.8 64.5 %copy-start.28 = (bf16[32,1088]{1,0:T(8,128)(2,1)S(1)}, bf16[32,1088]{1,0:T(8,128)(2,1)}, u32[]{:S(2)}) copy-start(bf16[32,1088]{1,0:T(8,128)(2,1)} %copy-done.27) | copy-start | bytes 208900
  169.8 65.3 %copy-start.26 = (bf16[32,1088]{1,0:T(8,128)(2,1)S(1)}, bf16[32,1088]{1,0:T(8,128)(2,1)}, u32[]{:S(2)}) copy-start(bf16[32,1088]{1,0:T(8,128)(2,1)} %get-tuple-element.41) | copy-start | bytes 208900
  169.8 63.0 %reduce-scatter.18.cloned.1.call-start = ((), (), s32[]{:S(2)}) async-start(), calls=%async_computation.10 | async-start | bytes 368640 | tf_op jit(solution)/shard_map/reduce_scatter | solution.py:100
  206.2 5.2 copy-start.15
  212.5 160.3 %all-gather.10.cloned.1.call-start = ((), (), s32[]{:S(2)}) async-start(), calls=%async_computation.11 | async-start | bytes 2433024 | tf_op jit(solution)/shard_map/all_gather | solution.py:264
  213.1 303.3 %all-gather.12.cloned.1.call-start = ((), (), s32[]{:S(2)}) async-start(), calls=%async_computation.12 | async-start | bytes 2433024 | tf_op jit(solution)/shard_map/all_gather | solution.py:265
  232.9 329.5 %reduce-scatter.16.cloned.1.call-start = ((), (), s32[]{:S(2)}) async-start(), calls=%async_computation.8 | async-start | bytes 348160 | tf_op jit(solution)/shard_map/reduce_scatter | solution.py:203
  372.7 249.4 %all-reduce.10.cloned.1.call-start = ((), (), s32[]{:S(2)}) async-start(), calls=%async_computation.13 | async-start | bytes 7241728
  516.3 4.3 copy-start.39
  516.3 4.3 copy-start.51
  527.4 18.1 %copy-start.41 = (f32[272]{0:T(512)S(1)}, f32[272]{0:T(512)}, u32[]{:S(2)}) copy-start(f32[272]{0:T(512)} %copy-done.40) | copy-start | bytes 3268
  549.0 3.5 copy-start.5
  549.1 3.5 copy-start.24
  549.1 3.5 copy-start.46
  549.1 3.5 copy-start.53
  549.1 115.3 %reduce-scatter.20.cloned.1.call-start = ((), (), s32[]{:S(2)}) async-start(), calls=%async_computation.14 | async-start | bytes 1880064
  552.5 170.5 %reduce-scatter.22.cloned.1.call-start = ((), (), s32[]{:S(2)}) async-start(), calls=%async_computation.15 | async-start | bytes 5640192
  555.8 226.0 %reduce-scatter.24.cloned.1.call-start = ((), (), s32[]{:S(2)}) async-start(), calls=%async_computation.16 | async-start | bytes 5640192
  560.1 4.0 copy-start.8
  560.1 18.6 %copy-start.42 = (f32[1088]{0:T(1024)S(1)}, f32[1088]{0:T(1024)}, u32[]{:S(2)}) copy-start(f32[1088]{0:T(1024)} %param.20) | copy-start | bytes 13060
  560.1 18.6 %copy-start.58 = (f32[128]{0:T(128)S(1)}, f32[128]{0:T(128)}, u32[]{:S(2)}) copy-start(f32[128]{0:T(128)} %copy-done.57) | copy-start | bytes 1540
  560.1 18.6 %copy-start.60 = (f32[128]{0:T(128)S(1)}, f32[128]{0:T(128)}, u32[]{:S(2)}) copy-start(f32[128]{0:T(128)} %copy-done.59) | copy-start | bytes 1540
  564.1 16.5 %copy-start.64 = (f32[1088]{0:T(1024)S(1)}, f32[1088]{0:T(1024)}, u32[]{:S(2)}) copy-start(f32[1088]{0:T(1024)} %get-tuple-element.57) | copy-start | bytes 13060
  564.7 217.2 %copy-start.1 = (bf16[1088,1088]{1,0:T(8,128)(2,1)S(1)}, bf16[1088,1088]{1,0:T(8,128)(2,1)}, u32[]{:S(2)}) copy-start(bf16[1088,1088]{1,0:T(8,128)(2,1)} %param.31) | copy-start | bytes 7102468
  (21 other events, 37.8 us)
Sparse Core Ops, SparseCore 0:
  15.3 26.9 reduce-scatter.13
  45.1 57.0 all-gather.7
  170.0 36.1 all-reduce.7
  212.6 20.2 reduce-scatter.17
  235.5 55.3 all-gather.9
  293.6 56.1 all-gather.11
  372.8 17.5 reduce-scatter.15
  549.2 72.8 all-reduce.9
  626.0 38.3 reduce-scatter.19
  668.3 54.7 reduce-scatter.21
  727.1 54.7 reduce-scatter.23
